TPU v7x, 32 devices: a whole 2x2x4 slice. The times are simulated.
32 devices in a mesh: replica: 8 (over z, y), fsdp: 4 (over x, core).
Axes of the slice: x: 2, y: 2, z: 4, core: 2. Of those that a mesh axis runs over, the one named last changes fastest.
Arguments:
- inner_weights: bfloat16 [8, 4, 1024, 8192], P('replica', None, 'fsdp'), may hold values from -6 to 6
- snapshot: bfloat16 [1024, 8192], P('fsdp'), may hold values from -6 to 6
- momentum: float32 [1024, 8192], P('fsdp', 'replica'), may hold values from -6 to 6
- rand_bits: int32 [8, 1024, 8192], P('replica', 'fsdp'), may hold values from 0 to 4095
- fragment: int32 [1], replicated, may hold values from 0 to 3
Outputs:
- new_snapshot: bfloat16 [1024, 8192], P('fsdp')
- new_momentum: float32 [1024, 8192], P('fsdp', 'replica')
- new_inner: bfloat16 [8, 4, 1024, 8192], P('replica', None, 'fsdp')
Inputs may be any that keep to these rules, and one draw needn't show every extreme that they name: fragment[0] is one of 0, 1, 2, 3, the fragment of the window that syncs.
All inputs are finite; a program needn't handle non-finite values.
Results may differ from a plain program's by a relative error of at most 0.0075.
Values may be sent and summed in bfloat16 or wider, within the bound.
A program may use at most 128 MiB of HBM per device.

v0:
```python
import jax
import jax.numpy as jnp
from jax import lax
from jax.sharding import PartitionSpec as P

momentum_coef = 0.9
outer_rate = 0.7
blend_keep = 0.5
grid_scale = 4.0
bit_levels = 4096.0


def stochastic_grid(snapshot, chosen, rand_bits):
    scaled = grid_scale * (snapshot.astype(jnp.float32) - chosen.astype(jnp.float32))
    lower = jnp.floor(scaled)
    raised = jnp.where(
        rand_bits.astype(jnp.float32) < bit_levels * (scaled - lower), 1.0, 0.0
    ).astype(jnp.float32)
    return ((lower + raised) / grid_scale).astype(jnp.bfloat16)


def outer_update(summed, replicas, momentum, snap_part):
    grad = summed / replicas
    moment_next = momentum_coef * momentum + grad
    snap_next = (
        snap_part.astype(jnp.float32) - outer_rate * (grad + momentum_coef * moment_next)
    ).astype(jnp.bfloat16)
    return (moment_next, snap_next)


def body(inner_weights, snapshot, momentum, rand_bits, fragment):
    fragment_id = fragment[0]
    chosen = lax.dynamic_index_in_dim(inner_weights[0], fragment_id, 0, keepdims=False)
    rounded = stochastic_grid(snapshot, chosen, rand_bits[0]).astype(jnp.float32)
    replicas = lax.axis_size("replica")
    share_cols = momentum.shape[1]
    offset = lax.axis_index("replica") * share_cols
    snap_cols = lax.dynamic_slice_in_dim(snapshot, offset, share_cols, 1)
    summed = lax.psum_scatter(
        rounded.astype(jnp.bfloat16), "replica", scatter_dimension=1, tiled=True
    ).astype(jnp.float32)
    new_momentum, snap_share = outer_update(summed, replicas, momentum, snap_cols)
    new_snapshot = lax.all_gather(snap_share, "replica", axis=1, tiled=True)
    blended = (
        blend_keep * chosen.astype(jnp.float32)
        + (1.0 - blend_keep) * new_snapshot.astype(jnp.float32)
    ).astype(jnp.bfloat16)
    picked = lax.broadcasted_iota(jnp.int32, (1, inner_weights.shape[1], 1, 1), 1) == fragment_id
    new_inner = jnp.where(picked, blended[None, None], inner_weights)
    return (new_snapshot, new_momentum, new_inner)


def solution(mesh):
    placed = (
        P("replica", None, "fsdp", None),
        P("fsdp", None),
        P("fsdp", "replica"),
        P("replica", "fsdp", None),
        P(),
    )
    return jax.shard_map(
        body,
        mesh=mesh,
        in_specs=placed,
        out_specs=(P("fsdp", None), P("fsdp", "replica"), P("replica", None, "fsdp", None)),
        check_vma=False,
    )
```

profile of v0, /device:TPU:0, one launch (start us, length us, event | category | flops | bytes accessed | tf_op | source)
XLA Modules:
  0.0 212.1 jit_solution(14411053555523721051)
XLA Ops:
  7.2 0.0 reduce-scatter.2.cloned.1.call-start
  7.9 0.0 copy-start.1
  7.9 8.9 %fusion.6 = bf16[256,8192]{1,0:T(8,128)(2,1)} fusion(s32[1,256,8192]{2,1,0:T(8,128)} %param.8, bf16[256,8192]{1,0:T(8,128)(2,1)} %param.6, bf16[1,4,256,8192]{3,2,1,0:T(8,128)(2,1)} %param.5, s32[]{:T(128)S(6)} %select_n.16), kind=kLoop, calls=%fused_computation.11 | loop fusion | flops 27262976 | bytes 20971524 | tf_op jit(solution)/shard_map/convert_element_type | solution.py:19
  16.8 0.0 reduce-scatter.2.cloned.1.call-update
  16.8 0.0 all-gather.2.cloned.1.call-start
  16.9 91.5 %reduce-scatter.2.cloned.1.call-done = bf16[256,1024]{1,0:T(8,128)(2,1)} async-done(((bf16[256,8192]{1,0:T(8,128)(2,1)}), bf16[256,1024]{1,0:T(8,128)(2,1)}) %reduce-scatter.2.cloned.1.call-update) | async-done | bytes 524304 | tf_op jit(solution)/shard_map/reduce_scatter | solution.py:39
  108.4 0.0 copy-done.1
  108.4 2.7 %subtract_convert_fusion = (bf16[256,1024]{1,0:T(8,128)(2,1)}, f32[256,1024]{1,0:T(8,128)}) fusion(bf16[256,1024]{1,0:T(8,128)(2,1)} %reduce-scatter.2.cloned.1.call-done, bf16[256,8192]{1,0:T(8,128)(2,1)} %param.6, s32[]{:T(128)S(6)} %select_n.15, f32[256,1024]{1,0:T(8,128)S(1)} %copy-done.1), kind=kLoop, calls=%fused_computation.12 | loop fusion | flops 2621440 | bytes 3670020 | tf_op jit(solution)/shard_map/convert_element_type | solution.py:27
  111.0 0.0 all-gather.2.cloned.1.call-update
  111.1 72.6 %all-gather.2.cloned.1.call-done = bf16[256,8192]{1,0:T(8,128)(2,1)} async-done(((bf16[256,1024]{1,0:T(8,128)(2,1)}), bf16[256,8192]{1,0:T(8,128)(2,1)}) %all-gather.2.cloned.1.call-update) | async-done | bytes 4194320 | tf_op jit(solution)/shard_map/all_gather | solution.py:43
  183.6 4.9 %fusion.2 = bf16[256,8192]{1,0:T(8,128)(2,1)S(1)} fusion(bf16[256,8192]{1,0:T(8,128)(2,1)} %all-gather.2.cloned.1.call-done, bf16[1,4,256,8192]{3,2,1,0:T(8,128)(2,1)} %param.5, s32[]{:T(128)S(6)} %select_n.16), kind=kLoop, calls=%fused_computation.7 | loop fusion | flops 10485760 | bytes 12582916 | tf_op jit(solution)/shard_map/convert_element_type | solution.py:47
  188.6 0.0 copy-start
  188.6 14.7 %broadcast_select_fusion = bf16[1,4,256,8192]{3,2,1,0:T(8,128)(2,1)} fusion(bf16[1,4,256,8192]{3,2,1,0:T(8,128)(2,1)} %param.5, pred[4]{0:T(512)(128)(4,1)S(1)} %iota_compare_fusion, bf16[256,8192]{1,0:T(8,128)(2,1)S(1)} %fusion.2), kind=kLoop, calls=%fused_computation | loop fusion | flops 8388608 | bytes 37748740 | tf_op jit(solution)/shard_map/jit(_where)/select_n | solution.py:49
  203.3 0.0 copy-done
  203.3 2.0 copy.10
  (1 shorter events, 0.0 us)
Async XLA Ops:
  7.2 101.2 %reduce-scatter.2.cloned.1.call-start = ((), (), s32[]{:S(2)}) async-start(), calls=%async_computation.1 | async-start | bytes 4718592 | tf_op jit(solution)/shard_map/reduce_scatter | solution.py:39
  7.9 100.5 %copy-start.1 = (f32[256,1024]{1,0:T(8,128)S(1)}, f32[256,1024]{1,0:T(8,128)}, u32[]{:S(2)}) copy-start(f32[256,1024]{1,0:T(8,128)} %param.7) | copy-start | bytes 3145732
  16.8 166.8 %all-gather.2.cloned.1.call-start = ((), (), s32[]{:S(2)}) async-start(), calls=%async_computation.2 | async-start | bytes 4718592 | tf_op jit(solution)/shard_map/all_gather | solution.py:43
  188.6 14.7 %copy-start = (bf16[256,8192]{1,0:T(8,128)(2,1)S(1)}, bf16[256,8192]{1,0:T(8,128)(2,1)}, u32[]{:S(2)}) copy-start(bf16[256,8192]{1,0:T(8,128)(2,1)} %all-gather.2.cloned.1.call-done) | copy-start | bytes 12582916
Sparse Core Ops, SparseCore 0:
  16.9 91.3 reduce-scatter.1
  111.2 72.4 all-gather.1
where the time goes:
time: 212 us
  waiting for transfers between devices  164 us (77%)
  other arithmetic  31.2 us (15%)
  between operations  14.7 us (7%)
    reduce_scatter x1, waiting for transfers between devices, body(): lax.psum_scatter(rounded.astype(jnp.bfloat16), 'replica', scatter_dimensi...  91.5 us
    all_gather x1, waiting for transfers between devices, body(): new_snapshot = lax.all_gather(snap_share, 'replica', axis=1, tiled=True)  72.6 us
    select_n x1, other arithmetic, body(): new_inner = jnp.where(picked, blended[None, None], inner_weights)  14.7 us
    convert_element_type x1, other arithmetic, stochastic_grid(): return ((lower + raised) / grid_scale).astype(jnp.bfloat16)  8.93 us
    convert_element_type x1, other arithmetic, body(): blended = (blend_keep * chosen.astype(jnp.float32) + (1.0 - blend_keep) *...  4.93 us
  transfers between devices with their start and end apart: 2, of which 2 were waited for; matrix products, arithmetic and copies ran while one was open for 0% of the time, Pallas kernels for 0%

commit v1 on v0

v1 whole, which is shorter than its diff:
```python
import functools

import jax
import jax.numpy as jnp
from jax import lax
from jax.experimental import pallas as pl
from jax.experimental.pallas import tpu as pltpu
from jax.sharding import PartitionSpec as P

momentum_coef = 0.9
outer_rate = 0.7
blend_keep = 0.5
grid_scale = 4.0
bit_levels = 4096.0
MESH = pl.DeviceIdType.MESH
CHUNK_ROWS = 16
OLDEST_FIRST = True
EXCHANGE_VMEM = 30 << 20
FINISH_VMEM = 10 << 20


def when(cond):
    if isinstance(cond, bool):
        return (lambda f: f()) if cond else (lambda f: None)
    return pl.when(cond)


def grid_of(n):
    inner = max(k for k in range(1, n + 1) if n % k == 0 and k * k <= n)
    return n // inner, inner


class Part:
    def __init__(self, bufs, sems, line1, line2, me, cols, width):
        self.own, self.r1, self.l1, self.r2, self.l2, self.res = bufs
        (self.s1, self.sr1, self.sl1, self.s2, self.sr2, self.sl2,
         self.g2, self.g2r, self.g2l, self.g1, self.g1r, self.g1l) = sems
        (self.p1, self.n1, self.d1) = line1
        (self.p2, self.n2, self.d2) = line2
        self.me, self.cols, self.width = me, cols, width
        self.top = self.n1 + self.n2 - 2
        self.last = 2 * self.top
        self.draining = False

    def send(self, src, dst, send_sem, recv_sem, delta):
        copy = pltpu.make_async_remote_copy(
            src_ref=src, dst_ref=dst, send_sem=send_sem, recv_sem=recv_sem,
            device_id={"replica": self.me + delta}, device_id_type=MESH,
        )
        if self.draining:
            copy.wait_send()
        else:
            copy.start()

    def arrive(self, dst, recv_sem):
        if not self.draining:
            pltpu.make_async_remote_copy(
                src_ref=dst, dst_ref=dst, send_sem=recv_sem, recv_sem=recv_sem,
                device_id={"replica": self.me}, device_id_type=MESH,
            ).wait_recv()

    def add1(self, c, q, recv):
        if not self.draining:
            for i in range(self.n2):
                self.own[c, q, i] = self.own[c, q, i] + recv[c, q, i]

    def add2(self, c, q, recv):
        if not self.draining:
            self.own[c, self.p1, q] = self.own[c, self.p1, q] + recv[c, q]

    def send1(self, c, q, right):
        recv, sem, delta = (self.r1, self.sr1, self.d1) if right else (self.l1, self.sl1, -self.d1)
        self.send(self.own.at[c, q], recv.at[c, q], self.s1.at[c, q], sem.at[c, q], delta)

    def send2(self, c, q, right):
        recv, sem, delta = (self.r2, self.sr2, self.d2) if right else (self.l2, self.sl2, -self.d2)
        self.send(self.own.at[c, self.p1, q], recv.at[c, q], self.s2.at[c, q], sem.at[c, q], delta)

    def gsend2(self, c, q, right):
        sem, delta = (self.g2r, self.d2) if right else (self.g2l, -self.d2)
        block = self.res.at[c, self.p1, q]
        self.send(block, block, sem.at[c, q], self.g2.at[c, q], delta)

    def gsend1(self, c, q1, q2, right):
        sem, delta = (self.g1r, self.d1) if right else (self.g1l, -self.d1)
        block = self.res.at[c, q1, q2]
        self.send(block, block, sem.at[c, q1, q2], self.g1.at[c, q1, q2], delta)

    def spread1(self, c, q2):
        p1 = self.p1
        when(p1 < self.n1 - 1)(lambda: self.gsend1(c, p1, q2, True))
        when(p1 > 0)(lambda: self.gsend1(c, p1, q2, False))

    def reduce_line(self, c, h, p, n, send, arrived, recvs, sems, add):
        right_recv, left_recv = recvs
        right_sem, left_sem = sems

        @when(p == h)
        def _():
            for q in range(n - 1, h - (h > 0), -1):
                if h > 0:
                    self.arrive(right_recv.at[c, q], right_sem.at[c, q])
                    if q > h or arrived:
                        add(c, q, right_recv)
                if q > h:
                    send(c, q, True)

        e = n - 1 - h

        @when(p == e)
        def _():
            for q in range(0, e + (h > 0)):
                if h > 0:
                    self.arrive(left_recv.at[c, q], left_sem.at[c, q])
                    if q < e or arrived:
                        add(c, q, left_recv)
                if q < e:
                    send(c, q, False)

    def hop1(self, s, c):
        if s < self.n1:
            self.reduce_line(c, s, self.p1, self.n1, self.send1, True, (self.r1, self.l1), (self.sr1, self.sl1), self.add1)

    def hop2(self, s, c):
        h = s - (self.n1 - 1)
        if 0 <= h < self.n2:
            self.reduce_line(c, h, self.p2, self.n2, self.send2, False, (self.r2, self.l2), (self.sr2, self.sl2), self.add2)

    def update(self, c, snap, mom, mom_next, acc, replicas, share):
        p1, p2 = self.p1, self.p2
        if not self.draining:
            acc[...] = self.own[c, p1, p2].astype(jnp.float32)

            @when(p2 > 0)
            def _():
                acc[...] += self.r2[c, p2].astype(jnp.float32)

            @when(p2 < self.n2 - 1)
            def _():
                acc[...] += self.l2[c, p2].astype(jnp.float32)

            start = self.me * share + self.cols
            if not isinstance(start, int):
                start = pl.multiple_of(start, 128)
            here = pl.ds(self.cols, self.width)
            grad = acc[...] / replicas
            moment = momentum_coef * mom[c, :, here] + grad
            mom_next[c, :, here] = moment
            base = snap[c, :, pl.ds(start, self.width)].astype(jnp.float32)
            self.res[c, p1, p2] = (base - outer_rate * (grad + momentum_coef * moment)).astype(jnp.bfloat16)
        when(p2 < self.n2 - 1)(lambda: self.gsend2(c, p2, True))
        when(p2 > 0)(lambda: self.gsend2(c, p2, False))
        self.spread1(c, p2)

    def gather(self, s, c):
        g = s - self.top
        p1, n1, p2, n2 = self.p1, self.n1, self.p2, self.n2
        if 1 <= g < n2:
            @when(p2 >= g)
            def _():
                self.arrive(self.res.at[c, p1, p2 - g], self.g2.at[c, p2 - g])
                when(p2 < n2 - 1)(lambda: self.gsend2(c, p2 - g, True))
                self.spread1(c, p2 - g)

            @when(p2 + g < n2)
            def _():
                self.arrive(self.res.at[c, p1, p2 + g], self.g2.at[c, p2 + g])
                when(p2 > 0)(lambda: self.gsend2(c, p2 + g, False))
                self.spread1(c, p2 + g)

        for h in range(n2):
            k = g - h
            if not 1 <= k < n1:
                continue
            for side in ((-1, 1) if h else (1,)):
                q2 = p2 + side * h

                @when(q2 >= 0 if side < 0 else q2 < n2)
                def _():
                    @when(p1 >= k)
                    def _():
                        self.arrive(self.res.at[c, p1 - k, q2], self.g1.at[c, p1 - k, q2])
                        when(p1 < n1 - 1)(lambda: self.gsend1(c, p1 - k, q2, True))

                    @when(p1 + k < n1)
                    def _():
                        self.arrive(self.res.at[c, p1 + k, q2], self.g1.at[c, p1 + k, q2])
                        when(p1 > 0)(lambda: self.gsend1(c, p1 + k, q2, False))


def exchange_kernel(dims, frag, inner, snapshot, momentum, bits, inner_v, res_a, res_b, mom_next, *scratch):
    outer, inner_n, chunks, share, wide = dims
    replicas = outer * inner_n
    frags = inner_v.shape[0]
    bbuf, snap, mom, acc_a, acc_b, wsem, bsem, ssem, msem = scratch[:9]
    bufs_a, bufs_b = (*scratch[9:14], res_a), (*scratch[14:19], res_b)
    sems_a, sems_b = scratch[19:31], scratch[31:43]
    me = lax.axis_index("replica")
    y, z = lax.rem(me, inner_n), lax.div(me, inner_n)
    line_y, line_z = (y, inner_n, 1), (z, outer, inner_n)
    part_a = Part(bufs_a, sems_a, line_y, line_z, me, 0, wide)
    part_b = Part(bufs_b, sems_b, line_z, line_y, me, wide, share - wide)
    parts = (part_a, part_b)

    def loads(c, slot):
        return (
            pltpu.make_async_copy(inner.at[0, :, c], inner_v.at[:, c], wsem.at[c]),
            pltpu.make_async_copy(bits.at[c], bbuf.at[slot], bsem.at[slot]),
            pltpu.make_async_copy(snapshot.at[c], snap.at[c], ssem.at[c]),
        )

    for copy in loads(0, 0):
        copy.start()
    mom_copy = pltpu.make_async_copy(momentum, mom, msem)
    mom_copy.start()

    barrier = pltpu.get_barrier_semaphore()
    count = 0
    for pos, n, step in (line_y, line_z):
        for delta, there in ((-step, pos > 0), (step, pos < n - 1)):
            @pl.when(there)
            def _():
                pl.semaphore_signal(barrier, inc=1, device_id={"replica": me + delta}, device_id_type=MESH)

            count = count + there.astype(jnp.int32)
    pl.semaphore_wait(barrier, count)
    mom_copy.wait()

    def round_chunk(c):
        slot = lax.rem(c, 2)

        @pl.when(c + 1 < chunks)
        def _():
            for copy in loads(c + 1, 1 - slot):
                copy.start()

        for copy in loads(c, slot):
            copy.wait()
        which = frag[0]
        for b in range(replicas):
            cols = slice(b * share, (b + 1) * share)
            chosen = inner_v[0, c, :, cols].astype(jnp.float32)
            for f in range(1, frags):
                chosen = jnp.where(which == f, inner_v[f, c, :, cols].astype(jnp.float32), chosen)
            scaled = grid_scale * (snap[c, :, cols].astype(jnp.float32) - chosen)
            lower = jnp.floor(scaled)
            raised = jnp.where(bbuf[slot, :, cols].astype(jnp.float32) < bit_levels * (scaled - lower), 1.0, 0.0)
            rounded = ((lower + raised) / grid_scale).astype(jnp.bfloat16)
            bz, by = b // inner_n, b % inner_n
            part_a.own[c, by, bz] = rounded[:, :wide]
            part_b.own[c, bz, by] = rounded[:, wide:]

    def stage(s, c):
        if s == 0 and not part_a.draining:
            round_chunk(c)
        for part in parts:
            part.hop1(s, c)
            part.hop2(s, c)
        if s == part_a.top:
            part_a.update(c, snap, mom, mom_next, acc_a, replicas, share)
            part_b.update(c, snap, mom, mom_next, acc_b, replicas, share)
        for part in parts:
            part.gather(s, c)

    stages = part_a.last + 1
    order = list(range(stages))
    if OLDEST_FIRST:
        order.reverse()

    def tick(t, carry):
        for s in order:
            c = t - s

            @pl.when(jnp.logical_and(c >= 0, c < chunks))
            def _():
                stage(s, c)

        return carry

    lax.fori_loop(0, chunks + stages - 1, tick, 0)

    part_a.draining = part_b.draining = True

    def drain(c, carry):
        for s in range(stages):
            stage(s, c)
        return carry

    lax.fori_loop(0, chunks, drain, 0)


def finish_kernel(frag, inner_v, res_a, res_b, mom_next, snap_out, mom_out, inner_out, snap_v, blend_v, mom_sem, pass_sem, snap_sem, blend_sem):
    frags, chunks = inner_v.shape[:2]
    n_y, n_z = res_a.shape[1], res_a.shape[2]
    wide = res_a.shape[4]
    share = wide + res_b.shape[4]
    which = frag[0]
    waits = [pltpu.make_async_copy(mom_next, mom_out, mom_sem)]
    for j in range(1, frags):
        other = lax.rem(which + j, frags)
        waits.append(pltpu.make_async_copy(inner_v.at[other], inner_out.at[0, other], pass_sem.at[j]))

    def puts(c):
        return (
            pltpu.make_async_copy(snap_v.at[c], snap_out.at[c], snap_sem.at[c]),
            pltpu.make_async_copy(blend_v.at[c], inner_out.at[0, which, c], blend_sem.at[c]),
        )

    for copy in waits:
        copy.start()

    def blend(c, carry):
        for bz in range(n_z):
            for by in range(n_y):
                first = (bz * n_y + by) * share
                for col, part in ((first, res_a[c, by, bz]), (first + wide, res_b[c, bz, by])):
                    cols = slice(col, col + part.shape[1])
                    snap_v[c, :, cols] = part
                    blend_v[c, :, cols] = (
                        blend_keep * inner_v[which, c, :, cols].astype(jnp.float32)
                        + (1.0 - blend_keep) * part.astype(jnp.float32)
                    ).astype(jnp.bfloat16)
        for copy in puts(c):
            copy.start()
        return carry

    lax.fori_loop(0, chunks, blend, 0)
    for copy in waits:
        copy.wait()

    def settle(c, carry):
        for copy in puts(c):
            copy.wait()
        return carry

    lax.fori_loop(0, chunks, settle, 0)


def body(inner_weights, snapshot, momentum, rand_bits, fragment):
    n = lax.axis_size("replica")
    outer, inner_n = grid_of(n)
    frags, rows, width = inner_weights.shape[1:]
    share = momentum.shape[1]
    wide = max(1, min(share // 128 - 1, round(0.6 * share / 128))) * 128
    narrow = share - wide
    chunks = rows // CHUNK_ROWS
    bf, f32 = jnp.bfloat16, jnp.float32
    dma = pltpu.SemaphoreType.DMA

    def bufs(n1, n2, w):
        full = (chunks, n1, n2, CHUNK_ROWS, w)
        line = (chunks, n2, CHUNK_ROWS, w)
        return [pltpu.VMEM(s, bf) for s in (full, full, full, line, line)]

    def sems(n1, n2):
        one, two, both = (chunks, n1), (chunks, n2), (chunks, n1, n2)
        return [dma(s) for s in (one,) * 3 + (two,) * 6 + (both,) * 3]

    scratch = [
        pltpu.VMEM((2, CHUNK_ROWS, width), jnp.int32),
        pltpu.VMEM((chunks, CHUNK_ROWS, width), bf),
        pltpu.VMEM((chunks, CHUNK_ROWS, share), f32),
        pltpu.VMEM((CHUNK_ROWS, wide), f32),
        pltpu.VMEM((CHUNK_ROWS, narrow), f32),
        dma((chunks,)), dma((2,)), dma((chunks,)), dma,
        *bufs(inner_n, outer, wide), *bufs(outer, inner_n, narrow),
        *sems(inner_n, outer), *sems(outer, inner_n),
    ]
    anywhere = pl.BlockSpec(memory_space=pl.ANY)
    in_vmem = pl.BlockSpec(memory_space=pltpu.VMEM)
    in_smem = pl.BlockSpec(memory_space=pltpu.SMEM)
    held = pl.pallas_call(
        functools.partial(exchange_kernel, (outer, inner_n, chunks, share, wide)),
        out_shape=(
            pltpu.VMEM((frags, chunks, CHUNK_ROWS, width), bf),
            pltpu.VMEM((chunks, inner_n, outer, CHUNK_ROWS, wide), bf),
            pltpu.VMEM((chunks, outer, inner_n, CHUNK_ROWS, narrow), bf),
            pltpu.VMEM((chunks, CHUNK_ROWS, share), f32),
        ),
        in_specs=[in_smem] + [pl.BlockSpec(memory_space=pltpu.HBM)] * 4,
        out_specs=(in_vmem,) * 4,
        scratch_shapes=scratch,
        compiler_params=pltpu.CompilerParams(
            collective_id=0, has_side_effects=True, vmem_limit_bytes=EXCHANGE_VMEM
        ),
        name="exchange",
    )(
        fragment,
        inner_weights.reshape(1, frags, chunks, CHUNK_ROWS, width),
        snapshot.reshape(chunks, CHUNK_ROWS, width),
        momentum.reshape(chunks, CHUNK_ROWS, share),
        rand_bits.reshape(chunks, CHUNK_ROWS, width),
    )

    new_snapshot, new_momentum, new_inner = pl.pallas_call(
        finish_kernel,
        in_specs=[in_smem] + [in_vmem] * 4,
        out_specs=(anywhere,) * 3,
        out_shape=(
            jax.ShapeDtypeStruct((chunks, CHUNK_ROWS, width), bf),
            jax.ShapeDtypeStruct((chunks, CHUNK_ROWS, share), f32),
            jax.ShapeDtypeStruct((1, frags, chunks, CHUNK_ROWS, width), bf),
        ),
        scratch_shapes=[
            pltpu.VMEM((chunks, CHUNK_ROWS, width), bf),
            pltpu.VMEM((chunks, CHUNK_ROWS, width), bf),
            dma, dma((frags,)), dma((chunks,)), dma((chunks,)),
        ],
        compiler_params=pltpu.CompilerParams(vmem_limit_bytes=FINISH_VMEM),
        name="finish",
    )(fragment, *held)
    return new_snapshot.reshape(rows, width), new_momentum.reshape(rows, share), new_inner.reshape(inner_weights.shape)


def solution(mesh):
    placed = (
        P("replica", None, "fsdp", None),
        P("fsdp", None),
        P("fsdp", "replica"),
        P("replica", "fsdp", None),
        P(),
    )
    return jax.shard_map(
        body,
        mesh=mesh,
        in_specs=placed,
        out_specs=(P("fsdp", None), P("fsdp", "replica"), P("replica", None, "fsdp", None)),
        check_vma=False,
    )
```

time: 212 us -> 121 us (0.57)
  waiting for transfers between devices: 164 us -> 0 us
  Pallas kernels: 0 us -> 118 us
  other arithmetic: 31.2 us -> 0 us
  between operations: 14.7 us -> 1.29 us
    pallas_call x0 -> x2, Pallas kernels: none -> 118 us  [the longest x1 111 us: body(): pl.pallas_call(functools.partial(exchange_kernel, (outer, inner_n, chunks...]
    reduce_scatter x1 -> x0, waiting for transfers between devices: 91.5 us -> none  [body(): lax.psum_scatter(rounded.astype(jnp.bfloat16), 'replica', scatter_dimensi...]
    all_gather x1 -> x0, waiting for transfers between devices: 72.6 us -> none  [body(): new_snapshot = lax.all_gather(snap_share, 'replica', axis=1, tiled=True)]
    convert_element_type x3 -> x0, other arithmetic: 16.5 us -> none  [the longest x1 8.93 us: stochastic_grid(): return ((lower + raised) / grid_scale).astype(jnp.bfloat16)]
    select_n x1 -> x0, other arithmetic: 14.7 us -> none  [body(): new_inner = jnp.where(picked, blended[None, None], inner_weights)]
  transfers between devices with their start and end apart: 2 -> 0, of which waited for: 2 -> 0; matrix products, arithmetic and copies ran while one was open for 0% -> 0% of each run, Pallas kernels for 0% -> 0%
where the time goes in v1:
time: 121 us
  Pallas kernels  118 us (98%)
  between operations  1.29 us (1%)
  local copies, waits for them, and re-layouts  1.22 us (1%)
    pallas_call x1, Pallas kernels, body(): pl.pallas_call(functools.partial(exchange_kernel, (outer, inner_n, chunks...  111 us
    pallas_call x1, Pallas kernels, body(): pl.pallas_call(finish_kernel, in_specs=[in_smem] + [in_vmem] * 4, out_spe...  7.69 us

profile of v1, /device:TPU:0, one launch (start us, length us, event | category | flops | bytes accessed | tf_op | source)
XLA Modules:
  0.0 121.0 jit_solution(8446733012501625128)
XLA Ops:
  1.3 0.0 copy-start
  1.3 1.2 %copy-done = f32[256,1024]{1,0:T(8,128)S(1)} copy-done((f32[256,1024]{1,0:T(8,128)S(1)}, f32[256,1024]{1,0:T(8,128)}, u32[]{:S(2)}) %copy-start) | copy-done | bytes 1048600
  2.5 110.8 %exchange.1 = (bf16[4,16,16,8192]{3,2,1,0:T(8,128)(2,1)S(1)}, bf16[16,2,4,16,640]{4,3,2,1,0:T(8,128)(2,1)S(1)}, bf16[16,4,2,16,384]{4,3,2,1,0:T(8,128)(2,1)S(1)}, f32[16,16,1024]{2,1,0:T(8,128)S(1)}) custom-call(s32[1]{0:T(128)S(6)} %copy.8.frag, bf16[1,4,16,16,8192]{4,3,2,1,0:T(8,128)(2,1)} %bitcast.8, bf16[16,16,8192]{2,1,0:T(8,128)(2,1)} %bitcast.10, ...), custom_call_target="tpu_custom_call" | custom-call | tf_op jit(solution)/shard_map/exchange/pallas_call | solution.py:372
  113.3 7.7 %finish.1 = (bf16[16,16,8192]{2,1,0:T(8,128)(2,1)}, f32[16,16,1024]{2,1,0:T(8,128)}, bf16[1,4,16,16,8192]{4,3,2,1,0:T(8,128)(2,1)}) custom-call(s32[1]{0:T(128)S(6)} %copy.8.frag, bf16[4,16,16,8192]{3,2,1,0:T(8,128)(2,1)S(1)} %get-tuple-element.10.inner_v, bf16[16,2,4,16,640]{4,3,2,1,0:T(8,128)(2,1)S(1)} %get-tuple-element.11.res_a, ...), custom_call_target="tpu_custom_call" | custom-call | tf_op jit(solution)/shard_map/finish/pallas_call | solution.py:395
Async XLA Ops:
  1.3 1.2 %copy-start = (f32[256,1024]{1,0:T(8,128)S(1)}, f32[256,1024]{1,0:T(8,128)}, u32[]{:S(2)}) copy-start(f32[256,1024]{1,0:T(8,128)} %param.7) | copy-start | bytes 3145732

commit v2 on v1

--- a/solution.py
+++ b/solution.py
@@ -13,9 +13,9 @@
 grid_scale = 4.0
 bit_levels = 4096.0
 MESH = pl.DeviceIdType.MESH
-CHUNK_ROWS = 16
+CHUNK_ROWS = 32
 OLDEST_FIRST = True
-EXCHANGE_VMEM = 30 << 20
+EXCHANGE_VMEM = 42 << 20
 FINISH_VMEM = 10 << 20
 
 
@@ -31,7 +31,7 @@
 
 
 class Part:
-    def __init__(self, bufs, sems, line1, line2, me, cols, width):
+    def __init__(self, bufs, sems, line1, line2, me, cols, width, draining):
         self.own, self.r1, self.l1, self.r2, self.l2, self.res = bufs
         (self.s1, self.sr1, self.sl1, self.s2, self.sr2, self.sl2,
          self.g2, self.g2r, self.g2l, self.g1, self.g1r, self.g1l) = sems
@@ -40,7 +40,7 @@
         self.me, self.cols, self.width = me, cols, width
         self.top = self.n1 + self.n2 - 2
         self.last = 2 * self.top
-        self.draining = False
+        self.draining = draining
 
     def send(self, src, dst, send_sem, recv_sem, delta):
         copy = pltpu.make_async_remote_copy(
@@ -198,9 +198,13 @@
     me = lax.axis_index("replica")
     y, z = lax.rem(me, inner_n), lax.div(me, inner_n)
     line_y, line_z = (y, inner_n, 1), (z, outer, inner_n)
-    part_a = Part(bufs_a, sems_a, line_y, line_z, me, 0, wide)
-    part_b = Part(bufs_b, sems_b, line_z, line_y, me, wide, share - wide)
-    parts = (part_a, part_b)
+
+    def parts_at(r, draining):
+        at_y, at_z = (r % inner_n, inner_n, 1), (r // inner_n, outer, inner_n)
+        return (
+            Part(bufs_a, sems_a, at_y, at_z, r, 0, wide, draining),
+            Part(bufs_b, sems_b, at_z, at_y, r, wide, share - wide, draining),
+        )
 
     def loads(c, slot):
         return (
@@ -247,46 +251,58 @@
             raised = jnp.where(bbuf[slot, :, cols].astype(jnp.float32) < bit_levels * (scaled - lower), 1.0, 0.0)
             rounded = ((lower + raised) / grid_scale).astype(jnp.bfloat16)
             bz, by = b // inner_n, b % inner_n
-            part_a.own[c, by, bz] = rounded[:, :wide]
-            part_b.own[c, bz, by] = rounded[:, wide:]
-
-    def stage(s, c):
-        if s == 0 and not part_a.draining:
-            round_chunk(c)
+            bufs_a[0][c, by, bz] = rounded[:, :wide]
+            bufs_b[0][c, bz, by] = rounded[:, wide:]
+
+    def stage(s, c, parts):
         for part in parts:
             part.hop1(s, c)
             part.hop2(s, c)
-        if s == part_a.top:
-            part_a.update(c, snap, mom, mom_next, acc_a, replicas, share)
-            part_b.update(c, snap, mom, mom_next, acc_b, replicas, share)
+        if s == top:
+            parts[0].update(c, snap, mom, mom_next, acc_a, replicas, share)
+            parts[1].update(c, snap, mom, mom_next, acc_b, replicas, share)
         for part in parts:
             part.gather(s, c)
 
-    stages = part_a.last + 1
-    order = list(range(stages))
-    if OLDEST_FIRST:
-        order.reverse()
+    top = inner_n + outer - 2
+    stages = 2 * top + 1
+
+    def at_my_place(todo, draining):
+        for r in range(replicas):
+            pl.when(me == r)(functools.partial(todo, parts_at(r, draining)))
 
     def tick(t, carry):
-        for s in order:
-            c = t - s
-
-            @pl.when(jnp.logical_and(c >= 0, c < chunks))
-            def _():
-                stage(s, c)
-
+        def older(parts):
+            for s in (range(stages - 1, 0, -1) if OLDEST_FIRST else range(1, stages)):
+                c = t - s
+
+                @pl.when(jnp.logical_and(c >= 0, c < chunks))
+                def _():
+                    stage(s, c, parts)
+
+        if OLDEST_FIRST:
+            at_my_place(older, False)
+
+        @pl.when(t < chunks)
+        def _():
+            round_chunk(t)
+            at_my_place(lambda parts: stage(0, t, parts), False)
+
+        if not OLDEST_FIRST:
+            at_my_place(older, False)
         return carry
 
     lax.fori_loop(0, chunks + stages - 1, tick, 0)
 
-    part_a.draining = part_b.draining = True
-
-    def drain(c, carry):
-        for s in range(stages):
-            stage(s, c)
-        return carry
-
-    lax.fori_loop(0, chunks, drain, 0)
+    def drain_at(parts):
+        def drain(c, carry):
+            for s in range(stages):
+                stage(s, c, parts)
+            return carry
+
+        lax.fori_loop(0, chunks, drain, 0)
+
+    at_my_place(drain_at, True)
 
 
 def finish_kernel(frag, inner_v, res_a, res_b, mom_next, snap_out, mom_out, inner_out, snap_v, blend_v, mom_sem, pass_sem, snap_sem, blend_sem):

time: 121 us -> 110 us (0.909)
  Pallas kernels: 118 us -> 108 us
  local copies, waits for them, and re-layouts: 1.22 us -> 0 us
    pallas_call x1, Pallas kernels: 111 us -> 101 us  [body(): pl.pallas_call(functools.partial(exchange_kernel, (outer, inner_n, chunks...]
    unnamed x2 -> x0, local copies, waits for them, and re-layouts: 1.22 us -> none
where the time goes in v2:
time: 110 us; the launch traced here: 109 us
  Pallas kernels  108 us (98%)
  between operations  1.29 us (1%)
    pallas_call x1, Pallas kernels, body(): pl.pallas_call(functools.partial(exchange_kernel, (outer, inner_n, chunks...  101 us
    pallas_call x1, Pallas kernels, body(): pl.pallas_call(finish_kernel, in_specs=[in_smem] + [in_vmem] * 4, out_spe...  7.57 us

profile of v2, /device:TPU:0, one launch (start us, length us, event | category | flops | bytes accessed | tf_op | source)
XLA Modules:
  0.0 109.4 jit_solution(14180686015250665036)
XLA Ops:
  1.3 100.6 %exchange.1 = (bf16[4,8,32,8192]{3,2,1,0:T(8,128)(2,1)S(1)}, bf16[8,2,4,32,640]{4,3,2,1,0:T(8,128)(2,1)S(1)}, bf16[8,4,2,32,384]{4,3,2,1,0:T(8,128)(2,1)S(1)}, f32[8,32,1024]{2,1,0:T(8,128)S(1)}) custom-call(s32[1]{0:T(128)S(6)} %copy.8.frag, bf16[1,4,8,32,8192]{4,3,2,1,0:T(8,128)(2,1)} %bitcast.7, bf16[8,32,8192]{2,1,0:T(8,128)(2,1)} %bitcast.9, ...), custom_call_target="tpu_custom_call" | custom-call | tf_op jit(solution)/shard_map/exchange/pallas_call | solution.py:388
  101.8 7.6 %finish.1 = (bf16[8,32,8192]{2,1,0:T(8,128)(2,1)}, f32[8,32,1024]{2,1,0:T(8,128)}, bf16[1,4,8,32,8192]{4,3,2,1,0:T(8,128)(2,1)}) custom-call(s32[1]{0:T(128)S(6)} %copy.8.frag, bf16[4,8,32,8192]{3,2,1,0:T(8,128)(2,1)S(1)} %get-tuple-element.10.inner_v, bf16[8,2,4,32,640]{4,3,2,1,0:T(8,128)(2,1)S(1)} %get-tuple-element.11.res_a, ...), custom_call_target="tpu_custom_call" | custom-call | tf_op jit(solution)/shard_map/finish/pallas_call | solution.py:411
